TPU v7x, 32 devices: a whole 2x2x4 slice. The times are simulated.
32 devices in a mesh: groups: 2 (over x), tensor: 8 (over z, y), dp: 2 (over core).
Axes of the slice: x: 2, y: 2, z: 4, core: 2. Of those that a mesh axis runs over, the one named last changes fastest.
Arguments:
- inputs: bfloat16 [4, 256, 16384], P(('groups', 'dp'), None, 'tensor'), parts along dimension 0, may hold values from -6 to 6
- cross_w: bfloat16 [16384, 16384], P('dp', 'tensor'), may hold values from -0.046875 to 0.046875
- cross_b: float32 [16384], P('tensor'), may hold values from -3 to 3
- mix_weight: bfloat16 [128, 512], replicated, may hold values from -0.5 to 0.5
- mix_bias: float32 [512], replicated, may hold values from -3 to 3
- out_weight: bfloat16 [512, 128], replicated, may hold values from -0.25 to 0.25
- cotangent: bfloat16 [4, 256, 16384], P(('groups', 'dp'), 'tensor'), parts along dimension 0, may hold values from -12 to 12
Outputs:
- compressed: bfloat16 [4, 256, 16384], P(('groups', 'dp'), 'tensor'), parts along dimension 0
- grad_inputs: bfloat16 [4, 256, 16384], P(('groups', 'dp'), None, 'tensor'), parts along dimension 0
- grad_mix: float32 [256, 512], P('groups'), parts along dimension 0
- grad_mix_bias: float32 [1024], P('groups'), parts along dimension 0
- grad_out: float32 [1024, 128], P('groups'), parts along dimension 0
There are 2 independent parts, one for each index of `groups`. A program takes and returns all parts, laid end to end along the dimension named above; an argument that names none is the same for every part. Nothing has to cross between parts.
All inputs are finite; a program needn't handle non-finite values.
Results may differ from a plain program's by a relative error of at most 0.019.
Values may be sent and summed in bfloat16 or wider, within the bound.
No kernel may reach another device: no remote copies, remote signals or barrier semaphores. Data moves between devices by JAX's collectives and lax.ppermute only.
A program may use at most 256 MiB of HBM per device.

v0:
```python
import jax
import jax.numpy as jnp
from jax import lax
from jax.sharding import PartitionSpec as P

F = 128
E = 128
K = 128


def shards(inputs, cross_w, cross_b, mix_weight, mix_bias, out_weight, cotangent):
    local_rows = inputs[0]
    dp_count = lax.axis_size("dp")
    full_rows = lax.all_gather(local_rows, "tensor", axis=1, tiled=True)
    linear = jnp.dot(
        full_rows,
        lax.all_gather(cross_w, "dp", axis=0, tiled=True),
        preferred_element_type=jnp.float32,
    )
    linear = linear + cross_b
    base_rows = local_rows.astype(jnp.float32)
    crossed = (base_rows * linear + base_rows).astype(jnp.bfloat16)
    owned = lax.all_to_all(crossed, "tensor", split_axis=0, concat_axis=1, tiled=True)
    owned_count = owned.shape[0]
    grid_rows = owned.reshape(owned_count, F, E)
    gram_rows = (
        jnp.einsum("bfe,bge->bfg", grid_rows, grid_rows, preferred_element_type=jnp.float32) / E
    ).astype(jnp.bfloat16)
    pre_act = (
        jnp.einsum("bfg,gh->bfh", gram_rows, mix_weight, preferred_element_type=jnp.float32)
        + mix_bias
    )
    sigmoid_pre = jax.nn.sigmoid(pre_act)
    hidden = (pre_act * sigmoid_pre).astype(jnp.bfloat16)
    compressed = jnp.einsum(
        "bfh,hk->bfk", hidden, out_weight, preferred_element_type=jnp.float32
    ).astype(jnp.bfloat16)
    upstream = cotangent[0].reshape(owned_count, F, K)
    d_hidden = jnp.einsum("bfk,hk->bfh", upstream, out_weight, preferred_element_type=jnp.float32)
    out_term = jnp.einsum("bfh,bfk->hk", hidden, upstream, preferred_element_type=jnp.float32)
    d_pre = (d_hidden * sigmoid_pre * (1.0 + pre_act * (1.0 - sigmoid_pre))).astype(jnp.bfloat16)
    mix_term = jnp.einsum("bfg,bfh->gh", gram_rows, d_pre, preferred_element_type=jnp.float32)
    bias_term = jnp.sum(d_pre.astype(jnp.float32), axis=(0, 1))
    mix_sum, bias_sum, out_sum = (
        lax.psum(mix_term.astype(jnp.bfloat16), ("tensor", "dp")).astype(jnp.float32),
        lax.psum(bias_term.astype(jnp.bfloat16), ("tensor", "dp")).astype(jnp.float32),
        lax.psum(out_term.astype(jnp.bfloat16), ("tensor", "dp")).astype(jnp.float32),
    )
    row_total = owned_count * lax.axis_size("tensor") * dp_count
    d_gram = jnp.einsum("bfh,gh->bfg", d_pre, mix_weight, preferred_element_type=jnp.float32)
    grid_wide = grid_rows.astype(jnp.float32)
    d_grid = jnp.einsum("bfg,bge->bfe", d_gram + jnp.swapaxes(d_gram, 1, 2), grid_wide) / E
    d_owned = d_grid.astype(jnp.bfloat16).reshape(owned_count, F * E)
    d_crossed = lax.all_to_all(d_owned, "tensor", split_axis=1, concat_axis=0, tiled=True)
    d_crossed_wide = d_crossed.astype(jnp.float32)
    d_linear = (d_crossed_wide * base_rows).astype(jnp.bfloat16)
    contract = (((1,), (1,)), ((), ()))
    back_terms = lax.dot_general(
        d_linear,
        lax.all_gather(cross_w, "dp", axis=0, tiled=True),
        contract,
        preferred_element_type=jnp.float32,
    )
    back_sum = lax.psum_scatter(
        back_terms.astype(jnp.bfloat16), "tensor", scatter_dimension=1, tiled=True
    ).astype(jnp.float32)
    grad_inputs = (d_crossed_wide * (linear + 1.0) + back_sum).astype(jnp.bfloat16)
    return (
        compressed.reshape(1, owned_count, F * K),
        grad_inputs[None],
        mix_sum / row_total,
        bias_sum / row_total,
        out_sum / row_total,
    )


def solution(mesh):
    return jax.shard_map(
        shards,
        mesh=mesh,
        in_specs=(
            P(("groups", "dp"), None, "tensor"),
            P("dp", "tensor"),
            P("tensor"),
            P(),
            P(),
            P(),
            P(("groups", "dp"), "tensor", None),
        ),
        out_specs=(
            P(("groups", "dp"), "tensor", None),
            P(("groups", "dp"), None, "tensor"),
            P("groups", None),
            P("groups"),
            P("groups", None),
        ),
        check_vma=False,
    )
```

profile of v0, /device:TPU:0, one launch (start us, length us, event | category | flops | bytes accessed | tf_op | source)
XLA Modules:
  0.0 582.4 jit_solution(2011968667886465584)
XLA Ops:
  7.2 0.0 copy-start
  7.2 0.0 all-gather.6.cloned.1.call-start
  7.2 0.7 all-gather.6.cloned.1.call-update
  7.9 0.0 copy-start.2
  7.9 0.0 copy-start.11
  7.9 0.0 all-gather.4.cloned.1.call-start
  8.0 0.7 all-gather.4.cloned.1.call-update
  8.7 129.2 %all-gather.6.cloned.1.call-done = bf16[1,256,16384]{2,1,0:T(8,128)(2,1)} async-done(((bf16[1,256,2048]{2,1,0:T(8,128)(2,1)}), bf16[1,256,16384]{2,1,0:T(8,128)(2,1)}) %all-gather.6.cloned.1.call-update) | async-done | bytes 8388624 | tf_op jit(solution)/shard_map/all_gather | solution.py:14
  137.9 94.9 %all-gather.4.cloned.1.call-done = bf16[16384,2048]{1,0:T(8,128)(2,1)} async-done(((bf16[8192,2048]{1,0:T(8,128)(2,1)}), bf16[16384,2048]{1,0:T(8,128)(2,1)}) %all-gather.4.cloned.1.call-update) | async-done | bytes 67108880 | tf_op jit(solution)/shard_map/all_gather | solution.py:17
  232.7 0.0 copy-done.2
  232.7 29.4 %fusion.5 = (bf16[256,2048]{1,0:T(8,128)(2,1)}, f32[256,2048]{1,0:T(8,128)}) fusion(bf16[1,256,2048]{2,1,0:T(8,128)(2,1)S(1)} %copy-done.2, f32[2048]{0:T(1024)S(1)} %copy-done.11, bf16[16384,2048]{1,0:T(8,128)(2,1)} %all-gather.4.cloned.1.call-done, bf16[1,256,16384]{2,1,0:T(8,128)(2,1)} %all-gather.6.cloned.1.call-done), kind=kOutput, calls=%fused_computation.10 | convolution fusion | flops 17182490624 | bytes 79699968 | tf_op jit(solution)/shard_map/dot_general | solution.py:15
  262.2 5.8 all-to-all-start
  267.9 0.2 copy.19
  268.2 0.0 copy-start.12
  268.2 26.0 %all-to-all-done = bf16[8,32,2048]{2,1,0:T(8,128)(2,1)S(1)} async-done(((bf16[8,32,2048]{2,1,0:T(8,128)(2,1)}), bf16[8,32,2048]{2,1,0:T(8,128)(2,1)S(1)}, u32[]{:S(2)}, u32[]{:S(2)}) %all-to-all-start) | async-done | bytes 1048608 | tf_op jit(solution)/shard_map/all_to_all | solution.py:23
  294.2 0.6 copy.12
  294.7 0.5 reshape.29
  295.3 0.8 multiply_convert_fusion.3
  296.1 0.0 copy-start.5
  296.2 0.0 copy-start.10
  296.2 3.9 multiply_convert_fusion.1
  300.1 0.0 copy-done.5
  300.1 3.7 fusion.18
  303.8 2.0 copy-done.1
  305.7 1.2 fusion.14
  307.0 1.8 copy.13
  308.8 3.0 multiply_convert_fusion.2
  311.8 1.6 all_to_all.25
  313.4 1.5 copy.14
  315.0 3.8 all-to-all-start.1
  318.8 0.2 all-reduce.3.cloned.1.call-start
  319.0 3.7 fusion.10
  322.8 2.0 fusion.11
  324.7 0.0 all-reduce.3.cloned.1.call-update
  324.8 0.0 reduce-scatter.2.cloned.1.call-start
  324.8 20.7 %all-to-all-done.1 = bf16[32,8,2048]{2,0,1:T(8,128)(2,1)S(1)} async-done(((bf16[32,8,2048]{2,0,1:T(8,128)(2,1)}), bf16[32,8,2048]{2,0,1:T(8,128)(2,1)S(1)}, u32[]{:S(2)}, u32[]{:S(2)}) %all-to-all-start.1) | async-done | bytes 1048608 | tf_op jit(solution)/shard_map/all_to_all | solution.py:54
  345.5 0.4 fusion.6
  345.9 30.1 %convolution_convert_fusion = bf16[256,16384]{1,0:T(8,128)(2,1)} fusion(bf16[256,2048]{1,0:T(8,128)(2,1)S(1)} %fusion.6, bf16[16384,2048]{1,0:T(8,128)(2,1)} %all-gather.4.cloned.1.call-done), kind=kOutput, calls=%fused_computation | convolution fusion | flops 17184063488 | bytes 76546048 | tf_op jit(solution)/shard_map/dot_general | solution.py:58
  376.0 0.0 reduce-scatter.2.cloned.1.call-update
  376.0 3.4 convolution_convert_fusion.1
  379.4 1.3 reshape.30
  380.7 31.5 %psum.22 = bf16[512]{0:T(512)(128)(2,1)S(1)} all-reduce(bf16[512]{0:T(512)(128)(2,1)S(1)} %get-tuple-element.11), channel_id=1, replica_groups=mesh['groups'=2,'tensor'=8,'dp'=2] {'tensor','dp'}, use_global_device_ids=true, to_apply=%region_3.0 | all-reduce | flops 512 | bytes 2048 | tf_op jit(solution)/shard_map/psum | solution.py:46
  412.2 0.6 convert_multiply_fusion.4
  412.8 6.3 %all-reduce.3.cloned.1.call-done = (bf16[128,512]{1,0:T(8,128)(2,1)}, bf16[512,128]{1,0:T(8,128)(2,1)}) async-done(((bf16[128,512]{1,0:T(8,128)(2,1)}, bf16[512,128]{1,0:T(8,128)(2,1)}), (bf16[128,512]{1,0:T(8,128)(2,1)}, bf16[512,128]{1,0:T(8,128)(2,1)})) %all-reduce.3.cloned.1.call-update) | async-done | bytes 262160 | tf_op jit(solution)/shard_map/psum | solution.py:45
  419.1 1.6 convert_multiply_fusion.3
  420.8 1.6 convert_multiply_fusion.2
  422.4 150.2 %reduce-scatter.2.cloned.1.call-done = bf16[256,2048]{1,0:T(8,128)(2,1)} async-done(((bf16[256,16384]{1,0:T(8,128)(2,1)}), bf16[256,2048]{1,0:T(8,128)(2,1)}) %reduce-scatter.2.cloned.1.call-update) | async-done | bytes 1048592 | tf_op jit(solution)/shard_map/reduce_scatter | solution.py:64
  572.5 3.3 fusion.8
  (17 shorter events, 0.0 us)
Async XLA Ops:
  7.2 289.0 %copy-start = (bf16[128,512]{1,0:T(8,128)(2,1)S(1)}, bf16[128,512]{1,0:T(8,128)(2,1)}, u32[]{:S(2)}) copy-start(bf16[128,512]{1,0:T(8,128)(2,1)} %param.10) | copy-start | bytes 393220
  7.2 130.7 %all-gather.6.cloned.1.call-start = ((), (), s32[]{:S(2)}) async-start(), calls=%async_computation.5 | async-start | bytes 9437184 | tf_op jit(solution)/shard_map/all_gather | solution.py:14
  7.9 224.8 %copy-start.2 = (bf16[1,256,2048]{2,1,0:T(8,128)(2,1)S(1)}, bf16[1,256,2048]{2,1,0:T(8,128)(2,1)}, u32[]{:S(2)}) copy-start(bf16[1,256,2048]{2,1,0:T(8,128)(2,1)} %param.7) | copy-start | bytes 3145732
  7.9 224.8 %copy-start.11 = (f32[2048]{0:T(1024)S(1)}, f32[2048]{0:T(1024)}, u32[]{:S(2)}) copy-start(f32[2048]{0:T(1024)} %param.9) | copy-start | bytes 24580
  7.9 224.8 %all-gather.4.cloned.1.call-start = ((), (), s32[]{:S(2)}) async-start(), calls=%async_computation.3 | async-start | bytes 100663296 | tf_op jit(solution)/shard_map/all_gather | solution.py:17
  8.7 259.2 %copy-start.7 = (bf16[1,32,16384]{2,1,0:T(8,128)(2,1)S(1)}, bf16[1,32,16384]{2,1,0:T(8,128)(2,1)}, u32[]{:S(2)}) copy-start(bf16[1,32,16384]{2,1,0:T(8,128)(2,1)} %param.13) | copy-start | bytes 3145732
  262.2 32.0 %all-to-all-start = ((bf16[8,32,2048]{2,1,0:T(8,128)(2,1)}), bf16[8,32,2048]{2,1,0:T(8,128)(2,1)S(1)}, u32[]{:S(2)}, u32[]{:S(2)}) async-start(bf16[8,32,2048]{2,1,0:T(8,128)(2,1)} %bitcast.2), calls=%async_computation | async-start | bytes 2097152 | tf_op jit(solution)/shard_map/all_to_all | solution.py:23
  268.2 31.9 %copy-start.8 = (bf16[4,8,128,128]{3,2,1,0:T(8,128)(2,1)}, bf16[4,8,128,128]{3,2,1,0:T(8,128)(2,1)S(1)}, u32[]{:S(2)}) copy-start(bf16[4,8,128,128]{3,2,1,0:T(8,128)(2,1)S(1)} %copy.19) | copy-start | bytes 3145732
  268.2 27.9 %copy-start.12 = (f32[512]{0:T(512)S(1)}, f32[512]{0:T(512)}, u32[]{:S(2)}) copy-start(f32[512]{0:T(512)} %param.11) | copy-start | bytes 6148
  296.1 3.9 copy-start.5
  296.2 3.9 copy-start.10
  303.8 2.0 copy-start.1
  311.8 7.2 %copy-start.6 = (bf16[32,128,128]{2,1,0:T(8,128)(2,1)S(1)}, bf16[32,128,128]{2,1,0:T(8,128)(2,1)}, u32[]{:S(2)}) copy-start(bf16[32,128,128]{2,1,0:T(8,128)(2,1)} %copy-done.5) | copy-start | bytes 3145732
  315.0 7.8 %copy-start.9 = (bf16[4,8,128,128]{3,2,1,0:T(8,128)(2,1)S(1)}, bf16[4,8,128,128]{3,2,1,0:T(8,128)(2,1)}, u32[]{:S(2)}) copy-start(bf16[4,8,128,128]{3,2,1,0:T(8,128)(2,1)} %copy-done.8) | copy-start | bytes 3145732
  315.0 30.5 %all-to-all-start.1 = ((bf16[32,8,2048]{2,0,1:T(8,128)(2,1)}), bf16[32,8,2048]{2,0,1:T(8,128)(2,1)S(1)}, u32[]{:S(2)}, u32[]{:S(2)}) async-start(bf16[32,8,2048]{2,0,1:T(8,128)(2,1)} %copy.14), calls=%async_computation.1 | async-start | bytes 2097152 | tf_op jit(solution)/shard_map/all_to_all | solution.py:54
  318.8 100.4 %all-reduce.3.cloned.1.call-start = ((), (), s32[]{:S(2)}) async-start(), calls=%async_computation.6 | async-start | bytes 524288 | tf_op jit(solution)/shard_map/psum | solution.py:45
  319.0 3.8 copy-start.4
  322.8 22.8 %copy-start.3 = (bf16[1,256,2048]{2,1,0:T(8,128)(2,1)S(1)}, bf16[1,256,2048]{2,1,0:T(8,128)(2,1)}, u32[]{:S(2)}) copy-start(bf16[1,256,2048]{2,1,0:T(8,128)(2,1)} %param.7) | copy-start | bytes 3145732
  324.8 247.8 %reduce-scatter.2.cloned.1.call-start = ((), (), s32[]{:S(2)}) async-start(), calls=%async_computation.4 | async-start | bytes 9437184 | tf_op jit(solution)/shard_map/reduce_scatter | solution.py:64
Sparse Core Ops, SparseCore 0:
  10.2 127.6 all-gather.5
  139.4 93.2 all-gather.3
  324.9 94.2 all-reduce.2
  422.6 149.8 reduce-scatter.1
where the time goes:
time: 583 us; the launch traced here: 582 us
  waiting for transfers between devices  429 us (74%)
  matrix products  81.3 us (14%)
  blocking collectives  31.5 us (5%)
  between operations  13.9 us (2%)
  starting transfers between devices  9.88 us (2%)
  local copies, waits for them, and re-layouts  9.63 us (2%)
  other arithmetic  7.58 us (1%)
    reduce_scatter x1, waiting for transfers between devices, shards(): lax.psum_scatter(back_terms.astype(jnp.bfloat16), 'tensor', scatter_dimen...  150 us
    all_gather x1, waiting for transfers between devices, shards(): full_rows = lax.all_gather(local_rows, 'tensor', axis=1, tiled=True)  129 us
    all_gather x1, waiting for transfers between devices, shards(): lax.all_gather(cross_w, 'dp', axis=0, tiled=True)  94.9 us
    psum x1, blocking collectives, shards(): lax.psum(bias_term.astype(jnp.bfloat16), ('tensor', 'dp'))  31.5 us
    dot_general x1, matrix products, shards(): lax.dot_general(d_linear, lax.all_gather(cross_w, 'dp', axis=0, tiled=Tru...  30.1 us
    dot_general x1, matrix products, shards(): jnp.dot(full_rows, lax.all_gather(cross_w, 'dp', axis=0, tiled=True), pre...  29.4 us
    all_to_all x1, waiting for transfers between devices, shards(): lax.all_to_all(crossed, 'tensor', split_axis=0, concat_axis=1, tiled=True)  26 us
    all_to_all x1, waiting for transfers between devices, shards(): lax.all_to_all(d_owned, 'tensor', split_axis=1, concat_axis=0, tiled=True)  20.7 us
  transfers between devices with their start and end apart: 6, of which 6 were waited for; matrix products, arithmetic and copies ran while one was open for 8% of the time, Pallas kernels for 0%

commit v1 on v0

--- a/solution.py
+++ b/solution.py
@@ -8,10 +8,26 @@
 K = 128
 
 
+def gather_around(x, axis, dim):
+    ways, here, step = (lax.axis_size(axis), lax.axis_index(axis), x.shape[dim])
+    shape = [n * ways if d == dim else n for d, n in enumerate(x.shape)]
+    full = lax.dynamic_update_slice_in_dim(jnp.zeros(shape, x.dtype), x, here * step, axis=dim)
+    going_up = going_down = x
+    for far in range(1, ways // 2 + 1):
+        going_up = lax.ppermute(going_up, axis, [(d, (d + 1) % ways) for d in range(ways)])
+        full = lax.dynamic_update_slice_in_dim(full, going_up, (here - far) % ways * step, axis=dim)
+        if 2 * far < ways:
+            going_down = lax.ppermute(going_down, axis, [(d, (d - 1) % ways) for d in range(ways)])
+            full = lax.dynamic_update_slice_in_dim(
+                full, going_down, (here + far) % ways * step, axis=dim
+            )
+    return full
+
+
 def shards(inputs, cross_w, cross_b, mix_weight, mix_bias, out_weight, cotangent):
     local_rows = inputs[0]
     dp_count = lax.axis_size("dp")
-    full_rows = lax.all_gather(local_rows, "tensor", axis=1, tiled=True)
+    full_rows = gather_around(local_rows, "tensor", 1)
     linear = jnp.dot(
         full_rows,
         lax.all_gather(cross_w, "dp", axis=0, tiled=True),

time: 583 us -> 527 us (0.904)
  waiting for transfers between devices: 429 us -> 337 us
  starting transfers between devices: 9.88 us -> 27.4 us
  local copies, waits for them, and re-layouts: 9.63 us -> 25.6 us
    ppermute x0 -> x7, waiting for transfers between devices: none -> 134 us  [the longest x4 117 us: gather_around(): lax.ppermute(going_up, axis, [(d, (d + 1) % ways) for d in range(ways)])]
    all_gather x1 -> x0, waiting for transfers between devices: 129 us -> none  [shards(): full_rows = lax.all_gather(local_rows, 'tensor', axis=1, tiled=True)]
    all_gather x1, waiting for transfers between devices: 94.9 us -> 0.01 us  [shards(): lax.all_gather(cross_w, 'dp', axis=0, tiled=True)]
    ppermute x0 -> x7, starting transfers between devices: none -> 19.6 us  [the longest x4 10.4 us: gather_around(): lax.ppermute(going_up, axis, [(d, (d + 1) % ways) for d in range(ways)])]
    dynamic_update_slice x0 -> x8, local copies, waits for them, and re-layouts: none -> 11.2 us  [the longest x4 5.59 us: gather_around(): lax.dynamic_update_slice_in_dim(full, going_up, (here - far) % ways * ste...]
  transfers between devices with their start and end apart: 6 -> 12, of which waited for: 6 -> 8; matrix products, arithmetic and copies ran while one was open for 8% -> 12% of each run, Pallas kernels for 0% -> 0%
where the time goes in v1:
time: 527 us
  waiting for transfers between devices  337 us (64%)
  matrix products  83.8 us (16%)
  blocking collectives  31.4 us (6%)
  starting transfers between devices  27.4 us (5%)
  local copies, waits for them, and re-layouts  25.6 us (5%)
  between operations  13.9 us (3%)
  other arithmetic  7.59 us (1%)
    reduce_scatter x1, waiting for transfers between devices, shards(): lax.psum_scatter(back_terms.astype(jnp.bfloat16), 'tensor', scatter_dimen...  150 us
    ppermute x4, waiting for transfers between devices, gather_around(): lax.ppermute(going_up, axis, [(d, (d + 1) % ways) for d in range(ways)])  117 us
    psum x1, blocking collectives, shards(): lax.psum(bias_term.astype(jnp.bfloat16), ('tensor', 'dp'))  31.4 us
    dot_general x1, matrix products, shards(): lax.dot_general(d_linear, lax.all_gather(cross_w, 'dp', axis=0, tiled=Tru...  30 us
    dot_general x1, matrix products, shards(): jnp.dot(full_rows, lax.all_gather(cross_w, 'dp', axis=0, tiled=True), pre...  29.5 us
    all_to_all x1, waiting for transfers between devices, shards(): lax.all_to_all(crossed, 'tensor', split_axis=0, concat_axis=1, tiled=True)  25.7 us
    all_to_all x1, waiting for transfers between devices, shards(): lax.all_to_all(d_owned, 'tensor', split_axis=1, concat_axis=0, tiled=True)  18.3 us
    ppermute x3, waiting for transfers between devices, gather_around(): lax.ppermute(going_down, axis, [(d, (d - 1) % ways) for d in range(ways)])  16.7 us
  transfers between devices with their start and end apart: 12, of which 8 were waited for; matrix products, arithmetic and copies ran while one was open for 12% of the time, Pallas kernels for 0%

profile of v1, /device:TPU:0, one launch (start us, length us, event | category | flops | bytes accessed | tf_op | source)
XLA Modules:
  0.0 526.6 jit_solution(17702255818214254524)
XLA Ops:
  7.2 0.7 all-gather.2.cloned.1.call-update
  8.4 3.0 collective-permute-start
  11.4 3.0 collective-permute-start.1
  14.5 41.8 %collective-permute-done = bf16[256,2048]{1,0:T(8,128)(2,1)S(1)} collective-permute-done((bf16[256,2048]{1,0:T(8,128)(2,1)S(1)}, bf16[256,2048]{1,0:T(8,128)(2,1)S(1)}, u32[]{:S(2)}, u32[]{:S(2)}) %collective-permute-start) | collective-permute-done | bytes 1048608 | tf_op jit(solution)/shard_map/ppermute | solution.py:17
  56.3 2.5 collective-permute-start.2
  58.8 3.1 collective-permute-start.3
  61.9 40.9 %collective-permute-done.2 = bf16[256,2048]{1,0:T(8,128)(2,1)} collective-permute-done((bf16[256,2048]{1,0:T(8,128)(2,1)S(1)}, bf16[256,2048]{1,0:T(8,128)(2,1)}, u32[]{:S(2)}, u32[]{:S(2)}) %collective-permute-start.2) | collective-permute-done | bytes 1048608 | tf_op jit(solution)/shard_map/ppermute | solution.py:17
  102.8 2.6 collective-permute-start.4
  105.4 4.2 broadcast_in_dim.8
  109.6 1.1 constant_dynamic-update-slice_fusion.7
  110.7 3.1 collective-permute-start.5
  113.8 1.1 constant_dynamic-update-slice_fusion.6
  114.8 34.2 %collective-permute-done.4 = bf16[256,2048]{1,0:T(8,128)(2,1)S(1)} collective-permute-done((bf16[256,2048]{1,0:T(8,128)(2,1)}, bf16[256,2048]{1,0:T(8,128)(2,1)S(1)}, u32[]{:S(2)}, u32[]{:S(2)}) %collective-permute-start.4) | collective-permute-done | bytes 1048608 | tf_op jit(solution)/shard_map/ppermute | solution.py:17
  149.0 2.4 collective-permute-start.6
  151.4 1.0 constant_dynamic-update-slice_fusion.5
  152.4 2.3 constant_dynamic-update-slice_fusion.4
  154.8 2.4 constant_dynamic-update-slice_fusion.3
  157.1 1.1 constant_dynamic-update-slice_fusion.2
  158.2 16.7 %collective-permute-done.5 = bf16[256,2048]{1,0:T(8,128)(2,1)S(1)} collective-permute-done((bf16[256,2048]{1,0:T(8,128)(2,1)}, bf16[256,2048]{1,0:T(8,128)(2,1)S(1)}, u32[]{:S(2)}, u32[]{:S(2)}) %collective-permute-start.5) | collective-permute-done | bytes 1048608 | tf_op jit(solution)/shard_map/ppermute | solution.py:20
  174.9 1.1 constant_dynamic-update-slice_fusion.1
  176.1 1.1 constant_dynamic-update-slice_fusion
  177.1 29.5 %fusion.1 = (bf16[256,2048]{1,0:T(8,128)(2,1)}, f32[256,2048]{1,0:T(8,128)}) fusion(bf16[1,256,2048]{2,1,0:T(8,128)(2,1)S(1)} %copy-done.2, f32[2048]{0:T(1024)S(1)} %copy-done.11, bf16[256,16384]{1,0:T(8,128)(2,1)} %constant_dynamic-update-slice_fusion, bf16[16384,2048]{1,0:T(8,128)(2,1)} %all-gather.2.cloned.1.call-done), kind=kOutput, calls=%fused_computation.8 | convolution fusion | flops 17182490624 | bytes 79699968 | tf_op jit(solution)/shard_map/dot_general | solution.py:31
  206.7 3.9 all-to-all-start
  210.8 25.7 %all-to-all-done = bf16[8,32,2048]{2,1,0:T(8,128)(2,1)S(1)} async-done(((bf16[8,32,2048]{2,1,0:T(8,128)(2,1)}), bf16[8,32,2048]{2,1,0:T(8,128)(2,1)S(1)}, u32[]{:S(2)}, u32[]{:S(2)}) %all-to-all-start) | async-done | bytes 1048608 | tf_op jit(solution)/shard_map/all_to_all | solution.py:39
  236.5 0.6 copy.12
  237.6 0.8 multiply_convert_fusion.3
  238.5 3.9 multiply_convert_fusion.1
  242.4 3.7 fusion.13
  246.1 2.0 copy-done.1
  248.1 1.2 fusion.9
  249.3 1.8 copy.13
  251.2 3.0 multiply_convert_fusion.2
  254.2 1.7 all_to_all.25
  255.9 1.5 copy.14
  257.4 3.6 all-to-all-start.1
  261.1 3.9 fusion.5
  265.0 4.1 fusion.6
  269.4 18.3 %all-to-all-done.1 = bf16[32,8,2048]{2,0,1:T(8,128)(2,1)S(1)} async-done(((bf16[32,8,2048]{2,0,1:T(8,128)(2,1)}), bf16[32,8,2048]{2,0,1:T(8,128)(2,1)S(1)}, u32[]{:S(2)}, u32[]{:S(2)}) %all-to-all-start.1) | async-done | bytes 1048608 | tf_op jit(solution)/shard_map/all_to_all | solution.py:70
  288.1 30.0 %convolution_convert_fusion = bf16[256,16384]{1,0:T(8,128)(2,1)} fusion(bf16[256,2048]{1,0:T(8,128)(2,1)S(1)} %fusion, bf16[16384,2048]{1,0:T(8,128)(2,1)} %all-gather.2.cloned.1.call-done), kind=kOutput, calls=%fused_computation | convolution fusion | flops 17184063488 | bytes 76546048 | tf_op jit(solution)/shard_map/dot_general | solution.py:74
  318.2 3.4 convolution_convert_fusion.1
  321.6 1.3 reshape.30
  322.9 31.4 %psum.22 = bf16[512]{0:T(512)(128)(2,1)S(1)} all-reduce(bf16[512]{0:T(512)(128)(2,1)S(1)} %get-tuple-element.11), channel_id=1, replica_groups=mesh['groups'=2,'tensor'=8,'dp'=2] {'tensor','dp'}, use_global_device_ids=true, to_apply=%region_3.4 | all-reduce | flops 512 | bytes 2048 | tf_op jit(solution)/shard_map/psum | solution.py:62
  354.3 0.6 convert_multiply_fusion.3
  354.9 8.3 %all-reduce.3.cloned.1.call-done = (bf16[128,512]{1,0:T(8,128)(2,1)}, bf16[512,128]{1,0:T(8,128)(2,1)}) async-done(((bf16[128,512]{1,0:T(8,128)(2,1)}, bf16[512,128]{1,0:T(8,128)(2,1)}), (bf16[128,512]{1,0:T(8,128)(2,1)}, bf16[512,128]{1,0:T(8,128)(2,1)})) %all-reduce.3.cloned.1.call-update) | async-done | bytes 262160 | tf_op jit(solution)/shard_map/psum | solution.py:61
  363.2 1.6 convert_multiply_fusion.1
  364.8 1.6 convert_multiply_fusion.2
  366.4 150.3 %reduce-scatter.2.cloned.1.call-done = bf16[256,2048]{1,0:T(8,128)(2,1)} async-done(((bf16[256,16384]{1,0:T(8,128)(2,1)}), bf16[256,2048]{1,0:T(8,128)(2,1)}) %reduce-scatter.2.cloned.1.call-update) | async-done | bytes 1048592 | tf_op jit(solution)/shard_map/reduce_scatter | solution.py:80
  516.7 3.4 fusion.3
  (37 shorter events, 2.1 us)
Async XLA Ops:
  7.2 231.3 %copy-start = (bf16[128,512]{1,0:T(8,128)(2,1)S(1)}, bf16[128,512]{1,0:T(8,128)(2,1)}, u32[]{:S(2)}) copy-start(bf16[128,512]{1,0:T(8,128)(2,1)} %param.10) | copy-start | bytes 393220
  7.2 1.3 copy-start.2
  7.2 169.9 %all-gather.2.cloned.1.call-start = ((), (), s32[]{:S(2)}) async-start(), calls=%async_computation.3 | async-start | bytes 100663296 | tf_op jit(solution)/shard_map/all_gather | solution.py:33
  8.4 47.9 %collective-permute-start = (bf16[256,2048]{1,0:T(8,128)(2,1)S(1)}, bf16[256,2048]{1,0:T(8,128)(2,1)S(1)}, u32[]{:S(2)}, u32[]{:S(2)}) collective-permute-start(bf16[256,2048]{1,0:T(8,128)(2,1)S(1)} %bitcast.61), channel_id=1, source_target_pairs={{0,2},{2,4},{4,6},{6,8},{8,10},{10,12},{12,14},{14,0},{1,3},{3,5},... | collective-permute-start | bytes 3145736 | tf_op jit(solution)/shard_map/ppermute | solution.py:17
  11.4 47.4 %collective-permute-start.1 = (bf16[256,2048]{1,0:T(8,128)(2,1)S(1)}, bf16[256,2048]{1,0:T(8,128)(2,1)S(1)}, u32[]{:S(2)}, u32[]{:S(2)}) collective-permute-start(bf16[256,2048]{1,0:T(8,128)(2,1)S(1)} %bitcast.62), channel_id=1, source_target_pairs={{0,14},{2,0},{4,2},{6,4},{8,6},{10,8},{12,10},{14,12},{1,15},{3,1}... | collective-permute-start | bytes 3145736 | tf_op jit(solution)/shard_map/ppermute | solution.py:20
  56.3 5.6 %copy-start.5 = (bf16[256,2048]{1,0:T(8,128)(2,1)}, bf16[256,2048]{1,0:T(8,128)(2,1)S(1)}, u32[]{:S(2)}) copy-start(bf16[256,2048]{1,0:T(8,128)(2,1)S(1)} %collective-permute-done) | copy-start | bytes 3145732
  56.3 46.5 %collective-permute-start.2 = (bf16[256,2048]{1,0:T(8,128)(2,1)S(1)}, bf16[256,2048]{1,0:T(8,128)(2,1)}, u32[]{:S(2)}, u32[]{:S(2)}) collective-permute-start(bf16[256,2048]{1,0:T(8,128)(2,1)S(1)} %collective-permute-done), channel_id=1, source_target_pairs={{0,2},{2,4},{4,6},{6,8},{8,10},{10,12},{12,14},{14,0},{1,3},{3,5},... | collective-permute-start | bytes 3145736 | tf_op jit(solution)/shard_map/ppermute | solution.py:17
  58.8 51.9 %collective-permute-start.3 = (bf16[256,2048]{1,0:T(8,128)(2,1)S(1)}, bf16[256,2048]{1,0:T(8,128)(2,1)}, u32[]{:S(2)}, u32[]{:S(2)}) collective-permute-start(bf16[256,2048]{1,0:T(8,128)(2,1)S(1)} %collective-permute-done.1), channel_id=1, source_target_pairs={{0,14},{2,0},{4,2},{6,4},{8,6},{10,8},{12,10},{14,12},{1,15},{3,1}... | collective-permute-start | bytes 3145736 | tf_op jit(solution)/shard_map/ppermute | solution.py:20
  102.8 46.2 %collective-permute-start.4 = (bf16[256,2048]{1,0:T(8,128)(2,1)}, bf16[256,2048]{1,0:T(8,128)(2,1)S(1)}, u32[]{:S(2)}, u32[]{:S(2)}) collective-permute-start(bf16[256,2048]{1,0:T(8,128)(2,1)} %collective-permute-done.2), channel_id=1, source_target_pairs={{0,2},{2,4},{4,6},{6,8},{8,10},{10,12},{12,14},{14,0},{1,3},{3,5},... | collective-permute-start | bytes 3145736 | tf_op jit(solution)/shard_map/ppermute | solution.py:17
  105.4 8.4 %copy-start.6 = (bf16[256,2048]{1,0:T(8,128)(2,1)S(1)}, bf16[256,2048]{1,0:T(8,128)(2,1)}, u32[]{:S(2)}) copy-start(bf16[256,2048]{1,0:T(8,128)(2,1)} %copy-done.5) | copy-start | bytes 3145732
  109.6 67.6 %copy-start.11 = (f32[2048]{0:T(1024)S(1)}, f32[2048]{0:T(1024)}, u32[]{:S(2)}) copy-start(f32[2048]{0:T(1024)} %param.9) | copy-start | bytes 24580
  110.7 64.2 %collective-permute-start.5 = (bf16[256,2048]{1,0:T(8,128)(2,1)}, bf16[256,2048]{1,0:T(8,128)(2,1)S(1)}, u32[]{:S(2)}, u32[]{:S(2)}) collective-permute-start(bf16[256,2048]{1,0:T(8,128)(2,1)} %collective-permute-done.3), channel_id=1, source_target_pairs={{0,14},{2,0},{4,2},{6,4},{8,6},{10,8},{12,10},{14,12},{1,15},{3,1}... | collective-permute-start | bytes 3145736 | tf_op jit(solution)/shard_map/ppermute | solution.py:20
  149.0 27.1 %collective-permute-start.6 = (bf16[256,2048]{1,0:T(8,128)(2,1)S(1)}, bf16[256,2048]{1,0:T(8,128)(2,1)S(1)}, u32[]{:S(2)}, u32[]{:S(2)}) collective-permute-start(bf16[256,2048]{1,0:T(8,128)(2,1)S(1)} %collective-permute-done.4), channel_id=1, source_target_pairs={{0,2},{2,4},{4,6},{6,8},{8,10},{10,12},{12,14},{14,0},{1,3},{3,5},... | collective-permute-start | bytes 3145736 | tf_op jit(solution)/shard_map/ppermute | solution.py:17
  177.1 33.4 %copy-start.7 = (bf16[1,32,16384]{2,1,0:T(8,128)(2,1)S(1)}, bf16[1,32,16384]{2,1,0:T(8,128)(2,1)}, u32[]{:S(2)}) copy-start(bf16[1,32,16384]{2,1,0:T(8,128)(2,1)} %param.13) | copy-start | bytes 3145732
  206.7 31.8 %copy-start.12 = (f32[512]{0:T(512)S(1)}, f32[512]{0:T(512)}, u32[]{:S(2)}) copy-start(f32[512]{0:T(512)} %param.11) | copy-start | bytes 6148
  206.7 29.8 %all-to-all-start = ((bf16[8,32,2048]{2,1,0:T(8,128)(2,1)}), bf16[8,32,2048]{2,1,0:T(8,128)(2,1)S(1)}, u32[]{:S(2)}, u32[]{:S(2)}) async-start(bf16[8,32,2048]{2,1,0:T(8,128)(2,1)} %bitcast.1), calls=%async_computation | async-start | bytes 2097152 | tf_op jit(solution)/shard_map/all_to_all | solution.py:39
  210.8 31.6 %copy-start.8 = (bf16[4,8,128,128]{3,2,1,0:T(8,128)(2,1)}, bf16[4,8,128,128]{3,2,1,0:T(8,128)(2,1)S(1)}, u32[]{:S(2)}) copy-start(bf16[4,8,128,128]{3,2,1,0:T(8,128)(2,1)S(1)} %copy.19) | copy-start | bytes 3145732
  238.5 3.9 copy-start.4
  238.5 3.9 copy-start.10
  246.1 2.0 copy-start.1
  254.2 10.8 %copy-start.9 = (bf16[4,8,128,128]{3,2,1,0:T(8,128)(2,1)S(1)}, bf16[4,8,128,128]{3,2,1,0:T(8,128)(2,1)}, u32[]{:S(2)}) copy-start(bf16[4,8,128,128]{3,2,1,0:T(8,128)(2,1)} %copy-done.8) | copy-start | bytes 3145732
  254.2 33.5 %copy-start.3 = (bf16[1,256,2048]{2,1,0:T(8,128)(2,1)S(1)}, bf16[1,256,2048]{2,1,0:T(8,128)(2,1)}, u32[]{:S(2)}) copy-start(bf16[1,256,2048]{2,1,0:T(8,128)(2,1)} %param.7) | copy-start | bytes 3145732
  257.4 30.3 %all-to-all-start.1 = ((bf16[32,8,2048]{2,0,1:T(8,128)(2,1)}), bf16[32,8,2048]{2,0,1:T(8,128)(2,1)S(1)}, u32[]{:S(2)}, u32[]{:S(2)}) async-start(bf16[32,8,2048]{2,0,1:T(8,128)(2,1)} %copy.14), calls=%async_computation.1 | async-start | bytes 2097152 | tf_op jit(solution)/shard_map/all_to_all | solution.py:70
  261.0 102.1 %all-reduce.3.cloned.1.call-start = ((), (), s32[]{:S(2)}) async-start(), calls=%async_computation.5 | async-start | bytes 524288 | tf_op jit(solution)/shard_map/psum | solution.py:61
  269.2 247.6 %reduce-scatter.2.cloned.1.call-start = ((), (), s32[]{:S(2)}) async-start(), calls=%async_computation.4 | async-start | bytes 9437184 | tf_op jit(solution)/shard_map/reduce_scatter | solution.py:80
Sparse Core Ops, SparseCore 0:
  9.6 97.7 all-gather.1
  269.3 93.8 all-reduce.2
  366.8 149.8 reduce-scatter.1
